TPU v7x, 32 devices: a whole 2x2x4 slice. The times are simulated.
32 devices in a mesh: row: 8 (over z, y), col: 4 (over x, core).
Axes of the slice: x: 2, y: 2, z: 4, core: 2. Of those that a mesh axis runs over, the one named last changes fastest.
Arguments:
- inv_interior: bfloat16 [64, 1024, 1024], P(('row', 'col')), may hold values from -1 to 3
- coupling: bfloat16 [64, 1024, 512], P(('row', 'col')), may hold values from -0.375 to 0.375
- boundary_stiff: bfloat16 [64, 512, 512], P(('row', 'col')), may hold values from -6 to 6
- mass_interior: float32 [64, 1024], P(('row', 'col')), may hold values from 0.5 to 2
- mass_boundary: float32 [64, 512], P(('row', 'col')), may hold values from 0.5 to 2
- block_map: int32 [64, 4], P(('row', 'col')), may hold values from 0 to 127, as said below
- modes: bfloat16 [16384, 1024], P('col', 'row'), may hold values from -0.046875 to 0.046875
Outputs:
- iface_stiff: bfloat16 [16384, 16384], P('row', 'col')
- iface_mass: bfloat16 [16384, 16384], P('row', 'col')
- reduced_stiff: float32 [1024, 1024], P(('row', 'col'))
- reduced_mass: float32 [1024, 1024], P(('row', 'col'))
- mass_diagonal: float32 [16384], P(('row', 'col'))
Inputs may be any that keep to these rules, and one draw needn't show every extreme that they name: Interface block p belongs to tile row p // 16 and tile column p // 32; the pair (block_map[s, a], block_map[s, b]) belongs to the tile of its row's tile row and its column's tile column. Over the 2 substructures of one device (aligned blocks of rows), no two triples (s, a, b) fall into the same tile, and in every draw some tile receives a pair from every device.
All inputs are finite; a program needn't handle non-finite values.
Results may differ from a plain program's by a relative error of at most 0.0058.
Values may be sent and summed in bfloat16 or wider, within the bound.
No kernel may reach another device: no remote copies, remote signals or barrier semaphores. Data moves between devices by JAX's collectives and lax.ppermute only.
A program may use at most 192 MiB of HBM per device.

v0:
```python
import jax
import jax.numpy as jnp
from jax import lax
from jax.sharding import PartitionSpec as P

BLK = 128


def broadcast(value, axis, source):
    kept = jnp.where(lax.axis_index(axis) == source, value, 0).astype(value.dtype)
    return lax.psum(kept, axis)


def condense(pieces):
    inverse, couple, stiffness, interior_mass, boundary_mass = pieces
    static_modes = (-jnp.dot(inverse, couple, preferred_element_type=jnp.float32)).astype(
        jnp.bfloat16
    )
    stiff_cond = stiffness.astype(jnp.float32) + jnp.dot(
        couple.T, static_modes, preferred_element_type=jnp.float32
    )
    weighted = (static_modes.astype(jnp.float32) * interior_mass[:, None]).astype(jnp.bfloat16)
    mass_cond = jnp.dot(static_modes.T, weighted, preferred_element_type=jnp.float32) + jnp.diag(
        boundary_mass
    )
    return jnp.stack([stiff_cond, mass_cond])


def body(inv_interior, coupling, boundary_stiff, mass_interior, mass_boundary, block_map, modes):
    row_count = lax.axis_size("row")
    col_count = lax.axis_size("col")
    device_count = row_count * col_count
    local_subs, interior_width, boundary_width = coupling.shape
    per_sub = boundary_width // BLK
    tile_cols = modes.shape[0]
    tile_rows = tile_cols * col_count // row_count
    mode_count = modes.shape[1] * row_count
    row_blocks = tile_rows // BLK
    col_blocks = tile_cols // BLK
    row_index = lax.axis_index("row")
    col_index = lax.axis_index("col")
    ratio_rows = row_count // col_count
    share_rows = tile_rows // col_count
    condensed = lax.map(
        condense, (inv_interior, coupling, boundary_stiff, mass_interior, mass_boundary)
    )
    blocks = condensed.reshape(local_subs, 2, per_sub, BLK, per_sub, BLK).transpose(
        0, 2, 4, 1, 3, 5
    )
    blocks = blocks.reshape(local_subs * per_sub * per_sub, 2, BLK, BLK)
    block_rows = jnp.broadcast_to(block_map[:, :, None], (local_subs, per_sub, per_sub)).reshape(-1)
    block_cols = jnp.broadcast_to(block_map[:, None, :], (local_subs, per_sub, per_sub)).reshape(-1)
    owner_index = block_rows // row_blocks * col_count + block_cols // col_blocks
    slot_index = block_rows % row_blocks * col_blocks + block_cols % col_blocks
    matches = owner_index[None, :] == jnp.arange(device_count, dtype=jnp.int32)[:, None]
    filled = jnp.any(matches, axis=1)
    chosen = jnp.argmax(matches, axis=1)
    outgoing = jnp.take(blocks, chosen, axis=0) * filled[:, None, None, None].astype(jnp.float32)
    targets = jnp.where(filled, jnp.take(slot_index, chosen), -1)
    arrived, arrived_slots = (
        lax.all_to_all(outgoing, ("row", "col"), split_axis=0, concat_axis=0, tiled=True),
        lax.all_to_all(targets, ("row", "col"), split_axis=0, concat_axis=0, tiled=True),
    )
    summed_blocks = jax.ops.segment_sum(
        arrived, jnp.maximum(arrived_slots, 0), num_segments=row_blocks * col_blocks
    )
    full_pair = summed_blocks.reshape(row_blocks, col_blocks, 2, BLK, BLK).transpose(2, 0, 3, 1, 4)
    full_pair = full_pair.reshape(2, tile_rows, tile_cols)
    holder = col_index == row_index // ratio_rows
    offset = row_index % ratio_rows * tile_rows
    column_ids = jnp.arange(tile_cols, dtype=jnp.int32)[None, :]
    row_ids = jnp.arange(tile_rows, dtype=jnp.int32)[:, None]
    on_diagonal = jnp.logical_and(column_ids == row_ids + offset, holder)
    mass_tile = full_pair[1]
    diag_local = jnp.sum(jnp.where(on_diagonal, mass_tile, jnp.float32(0.0)), axis=1)
    mass_share = lax.psum_scatter(diag_local, "col", scatter_dimension=0, tiled=True)
    stiff_tile = full_pair[0].astype(jnp.bfloat16)
    mass_off = jnp.where(on_diagonal, jnp.float32(0.0), mass_tile).astype(jnp.bfloat16)
    col_modes = lax.all_gather(modes, "row", axis=1, tiled=True)
    mode_slab = lax.dynamic_slice_in_dim(
        col_modes, row_index % ratio_rows * tile_rows, tile_rows, 0
    )
    row_modes = broadcast(mode_slab, "col", row_index // ratio_rows)
    right_side = jnp.concatenate(
        [
            jnp.dot(stiff_tile, col_modes, preferred_element_type=jnp.float32),
            jnp.dot(mass_off, col_modes, preferred_element_type=jnp.float32),
        ],
        1,
    )
    left_modes = row_modes.astype(jnp.float32)
    share_start = col_index * share_rows
    share_modes = lax.dynamic_slice_in_dim(left_modes, share_start, share_rows, 0)
    mass_part = lax.dynamic_slice(
        right_side, (share_start, jnp.int32(mode_count)), (share_rows, mode_count)
    )
    right_side = lax.dynamic_update_slice(
        right_side,
        mass_part + mass_share[:, None] * share_modes,
        (share_start, jnp.int32(mode_count)),
    )
    reduced = lax.psum_scatter(
        jnp.dot(
            left_modes.T,
            right_side,
            precision=lax.Precision.HIGHEST,
            preferred_element_type=jnp.float32,
        ),
        ("row", "col"),
        scatter_dimension=0,
        tiled=True,
    )
    return (stiff_tile, mass_off, reduced[:, :mode_count], reduced[:, mode_count:], mass_share)


def solution(mesh):
    return jax.shard_map(
        body,
        mesh=mesh,
        in_specs=(
            P(("row", "col"), None, None),
            P(("row", "col"), None, None),
            P(("row", "col"), None, None),
            P(("row", "col"), None),
            P(("row", "col"), None),
            P(("row", "col"), None),
            P("col", "row"),
        ),
        out_specs=(
            P("row", "col"),
            P("row", "col"),
            P(("row", "col"), None),
            P(("row", "col"), None),
            P(("row", "col")),
        ),
        check_vma=False,
    )
```

profile of v0, /device:TPU:0, one launch (start us, length us, event | category | flops | bytes accessed | tf_op | source)
XLA Modules:
  0.0 656.3 jit_solution(4957446809778439733)
XLA Ops:
  11.0 7.3 %all-to-all-start = ((s32[32,1,1]{2,1,0:T(1,128)}), s32[32,1,1]{2,1,0:T(1,128)S(1)}, u32[]{:S(2)}, u32[]{:S(2)}) async-start(s32[32,1,1]{2,1,0:T(1,128)} %copy.28), calls=%async_computation | async-start | bytes 32768 | tf_op jit(solution)/shard_map/all_to_all | solution.py:62
  18.3 14.7 %while.10 = (s32[]{:T(128)}, f32[2,2,512,512]{3,2,1,0:T(8,128)}, bf16[2,512,512]{2,1,0:T(8,128)(2,1)}, bf16[2,1024,512]{2,1,0:T(8,128)(2,1)}, bf16[2,1024,1024]{...) while((s32[]{:T(128)}, f32[2,2,512,512]{3,2,1,0:T(8,128)}, ...), condition=%wide.region_3.4_spmd, body=%wide.region_2.3_spmd.sunk | while | flops 2151940096 | bytes 60363024 | solution.py:44
  33.0 5.2 reshape.158
  38.2 4.8 copy.29
  43.0 5.0 gather_fusion.1
  48.0 5.2 select_multiply_fusion
  53.2 6.0 all-to-all-start.1
  62.8 171.5 %all-to-all-done.1 = f32[32,2,128,128]{3,2,1,0:T(8,128)} async-done(((f32[32,2,128,128]{3,2,1,0:T(8,128)}), f32[32,2,128,128]{3,2,1,0:T(8,128)}, u32[]{:S(2)}, u32[]{:S(2)}) %all-to-all-start.1) | async-done | bytes 4194336 | tf_op jit(solution)/shard_map/all_to_all | solution.py:61
  234.3 21.2 %broadcast_in_dim.82 = f32[512,2,128,128]{3,2,1,0:T(8,128)} broadcast(f32[]{:T(128)} %constant.133.clone.1), dimensions={} | broadcast | bytes 67108864 | tf_op jit(solution)/shard_map/broadcast_in_dim | solution.py:64
  255.6 9.7 %scatter_fusion = f32[512,2,128,128]{3,2,1,0:T(8,128)} fusion(f32[512,2,128,128]{3,2,1,0:T(8,128)} %broadcast_in_dim.82, s32[32]{0:T(128)S(1)} %maximum_reduce_fusion, f32[32,2,128,128]{3,2,1,0:T(8,128)} %all-to-all-done.1), kind=kCustom, calls=%fused_computation.2 | custom fusion | flops 1048576 | bytes 12583040 | tf_op jit(solution)/shard_map/scatter-add | solution.py:64
  265.3 27.9 %fusion.25 = (bf16[1,16,128,32,128]{4,2,0,3,1:T(8,128)(2,1)S(1)}, bf16[1,16,128,32,128]{4,2,0,3,1:T(8,128)(2,1)}) fusion(f32[2,16,128,32,128]{4,2,0,3,1:T(8,128)} %bitcast.12), kind=kLoop, calls=%fused_computation.64 | loop fusion | bytes 67108864 | tf_op jit(solution)/shard_map/slice | solution.py:74
  293.2 14.7 %copy.30 = bf16[1,16,128,32,128]{4,3,2,1,0:T(8,128)(2,1)S(1)} copy(bf16[1,16,128,32,128]{4,2,0,3,1:T(8,128)(2,1)} %get-tuple-element.62) | data formatting | bytes 33554432 | tf_op jit(solution)/shard_map/slice | solution.py:77
  307.9 11.0 %copy.37 = bf16[256,8,32,128]{3,1,2,0:T(8,128)(2,1)} copy(bf16[256,8,32,128]{3,2,1,0:T(8,128)(2,1)S(1)} %bitcast.76) | data formatting | bytes 33554432
  318.9 11.6 %copy.31 = bf16[1,16,128,32,128]{4,3,2,1,0:T(8,128)(2,1)} copy(bf16[1,16,128,32,128]{4,2,0,3,1:T(8,128)(2,1)S(1)} %get-tuple-element.61) | data formatting | bytes 33554432 | tf_op jit(solution)/shard_map/slice | solution.py:74
  330.5 14.6 %select_reduce_fusion = f32[16,128]{1,0:T(8,128)S(1)} fusion(s32[16,128]{1,0:T(8,128)S(1)} %add_add_fusion, s32[32,128]{1,0:T(8,128)S(1)} %multiply_add_fusion, pred[]{:T(512)S(6)} %eq.67, f32[2,16,128,32,128]{4,2,0,3,1:T(8,128)} %bitcast.12), kind=kLoop, calls=%fused_computation.28 | loop fusion | flops 33552384 | bytes 33587200 | tf_op jit(solution)/shard_map/reduce_sum | solution.py:75
  345.1 5.8 all-reduce
  350.9 21.1 %fusion.17 = bf16[2048,4096]{1,0:T(8,128)(2,1)} fusion(bf16[256,8,32,128]{3,2,1,0:T(8,128)(2,1)} %bitcast.75, s32[2048]{0:T(1024)S(1)} %iota_add_fusion, pred[]{:T(512)S(6)} %eq.67), kind=kLoop, calls=%fused_computation.26 | loop fusion | flops 25165824 | bytes 33562624 | tf_op jit(solution)/shard_map/convert_element_type | solution.py:78
  372.1 5.5 dynamic-slice_select_fusion
  377.8 21.7 %fusion.28 = f32[2048,1024]{0,1:T(8,128)S(1)} fusion(bf16[2048,4096]{1,0:T(8,128)(2,1)} %fusion.17, bf16[4096,1024]{0,1:T(8,128)(2,1)} %all-gather.2.cloned.1.call-done), kind=kOutput, calls=%fused_computation.67 | convolution fusion | flops 17179869184 | bytes 33554432 | tf_op jit(solution)/shard_map/dot_general | solution.py:87
  399.5 24.7 %fusion.27 = f32[2048,1024]{0,1:T(8,128)S(1)} fusion(bf16[2048,4096]{1,0:T(8,128)(2,1)} %bitcast.77, bf16[4096,1024]{0,1:T(8,128)(2,1)} %all-gather.2.cloned.1.call-done), kind=kOutput, calls=%fused_computation.66 | convolution fusion | flops 17179869184 | bytes 33554432 | tf_op jit(solution)/shard_map/dot_general | solution.py:86
  427.5 6.3 pad_maximum_fusion
  433.9 29.6 %all-reduce.3.cloned.1.call-done = bf16[2048,1024]{0,1:T(8,128)(2,1)} async-done(((bf16[2048,1024]{0,1:T(8,128)(2,1)}), bf16[2048,1024]{0,1:T(8,128)(2,1)}) %all-reduce.3.cloned.1.call-update) | async-done | bytes 4194320 | tf_op jit(solution)/shard_map/psum | solution.py:11
  467.3 30.5 %fusion.29 = f32[1024,2048]{1,0:T(8,128)} fusion(bf16[2048,1024]{0,1:T(8,128)(2,1)S(1)} %copy-done.5, f32[2048,2048]{0,1:T(8,128)} %fusion.21), kind=kOutput, calls=%fused_computation.68 | convolution fusion | flops 51539607552 | bytes 29360128 | tf_op jit(solution)/shard_map/dot_general | solution.py:103
  497.7 150.4 %reduce-scatter.2.cloned.1.call-done = f32[32,2048]{1,0:T(8,128)} async-done(((f32[1024,2048]{1,0:T(8,128)}), f32[32,2048]{1,0:T(8,128)}) %reduce-scatter.2.cloned.1.call-update) | async-done | bytes 262160 | tf_op jit(solution)/shard_map/reduce_scatter | solution.py:102
  (79 shorter events, 30.3 us)
Async XLA Ops:
  11.0 42.2 %all-to-all-start = ((s32[32,1,1]{2,1,0:T(1,128)}), s32[32,1,1]{2,1,0:T(1,128)S(1)}, u32[]{:S(2)}, u32[]{:S(2)}) async-start(s32[32,1,1]{2,1,0:T(1,128)} %copy.28), calls=%async_computation | async-start | bytes 32768 | tf_op jit(solution)/shard_map/all_to_all | solution.py:62
  18.3 3.3 copy-start.6
  18.3 3.3 copy-start.7
  18.4 4.2 copy-start.9
  18.4 4.2 copy-start.10
  18.4 5.0 copy-start.2
  23.6 2.0 copy-start.3
  25.7 3.3 copy-start.6
  25.7 3.3 copy-start.7
  25.7 4.2 copy-start.9
  25.7 4.2 copy-start.10
  25.7 5.0 copy-start.2
  31.0 2.0 copy-start.3
  48.0 11.2 %copy-start.4 = (bf16[4096,128]{1,0:T(8,128)(2,1)S(1)}, bf16[4096,128]{1,0:T(8,128)(2,1)}, u32[]{:S(2)}) copy-start(bf16[4096,128]{1,0:T(8,128)(2,1)} %param.15) | copy-start | bytes 3145732
  48.0 12.9 %copy-start.11 = (u32[32]{0:T(128)S(1)}, u32[32]{0:T(128)}, u32[]{:S(2)}) copy-start(u32[32]{0:T(128)} %constant.164) | copy-start | bytes 388
  53.2 181.1 %all-to-all-start.1 = ((f32[32,2,128,128]{3,2,1,0:T(8,128)}), f32[32,2,128,128]{3,2,1,0:T(8,128)}, u32[]{:S(2)}, u32[]{:S(2)}) async-start(f32[32,2,128,128]{3,2,1,0:T(8,128)} %select_multiply_fusion), calls=%async_computation.1 | async-start | bytes 8388608 | tf_op jit(solution)/shard_map/all_to_all | solution.py:61
  59.2 312.9 %all-gather.2.cloned.1.call-start = ((), (), s32[]{:S(2)}) async-start(), calls=%async_computation.3 | async-start | bytes 9437184 | tf_op jit(solution)/shard_map/all_gather | solution.py:79
  60.6 402.9 %all-reduce.3.cloned.1.call-start = ((), (), s32[]{:S(2)}) async-start(), calls=%async_computation.4 | async-start | bytes 8388608 | tf_op jit(solution)/shard_map/psum | solution.py:11
  350.9 112.6 %copy-start.8 = (f32[512]{0:T(512)}, f32[512]{0:T(512)S(1)}, u32[]{:S(2)}) copy-start(f32[512]{0:T(512)S(1)} %dynamic-slice.1) | copy-start | bytes 6148
  377.5 270.6 %reduce-scatter.2.cloned.1.call-start = ((), (), s32[]{:S(2)}) async-start(), calls=%async_computation.5 | async-start | bytes 8650752 | tf_op jit(solution)/shard_map/reduce_scatter | solution.py:102
  399.5 24.7 %copy-start = (f32[2048,1024]{0,1:T(8,128)}, f32[2048,1024]{0,1:T(8,128)S(1)}, u32[]{:S(2)}) copy-start(f32[2048,1024]{0,1:T(8,128)S(1)} %fusion.28) | copy-start | bytes 25165828
  424.2 3.3 copy-start.1
  463.5 3.8 copy-start.5
Sparse Core Ops, SparseCore 0:
  62.1 192.2 all-gather.1
  377.6 85.7 all-reduce.2
  497.9 150.1 reduce-scatter.1
where the time goes:
time: 657 us; the launch traced here: 656 us
  waiting for transfers between devices  352 us (54%)
  local copies, waits for them, and re-layouts  116 us (18%)
  matrix products  86.6 us (13%)
  other arithmetic  68.2 us (10%)
  between operations  14.6 us (2%)
  starting transfers between devices  13.8 us (2%)
    all_to_all x1, waiting for transfers between devices, body(): lax.all_to_all(outgoing, ('row', 'col'), split_axis=0, concat_axis=0, til...  172 us
    reduce_scatter x1, waiting for transfers between devices, body(): lax.psum_scatter(jnp.dot(left_modes.T, right_side, precision=lax.Precisio...  150 us
    slice x2, local copies, waits for them, and re-layouts, body(): mass_tile = full_pair[1]  39.5 us
    dot_general x1, matrix products, body(): jnp.dot(left_modes.T, right_side, precision=lax.Precision.HIGHEST, prefer...  30.5 us
    psum x1, waiting for transfers between devices, broadcast(): return lax.psum(kept, axis)  29.6 us
    dot_general x1, matrix products, body(): jnp.dot(stiff_tile, col_modes, preferred_element_type=jnp.float32)  24.7 us
    dot_general x1, matrix products, body(): jnp.dot(mass_off, col_modes, preferred_element_type=jnp.float32)  21.7 us
    broadcast_in_dim x1, local copies, waits for them, and re-layouts, body(): jax.ops.segment_sum(arrived, jnp.maximum(arrived_slots, 0), num_segments=...  21.2 us
  transfers between devices with their start and end apart: 5, of which 3 were waited for; matrix products, arithmetic and copies ran while one was open for 33% of the time, Pallas kernels for 0%

commit v1 on v0

--- a/solution.py
+++ b/solution.py
@@ -6,9 +6,15 @@
 BLK = 128
 
 
+def summed_here(value, mesh_axis):
+    parts = lax.all_gather(value, mesh_axis, axis=0, tiled=False)
+    result = parts.sum(axis=0)
+    return result
+
+
 def broadcast(value, axis, source):
     kept = jnp.where(lax.axis_index(axis) == source, value, 0).astype(value.dtype)
-    return lax.psum(kept, axis)
+    return summed_here(kept, axis)
 
 
 def condense(pieces):

time: 657 us -> 692 us (1.053)
  other arithmetic: 68.2 us -> 83.5 us
  matrix products: 86.6 us -> 95.9 us
  waiting for transfers between devices: 352 us -> 360 us
    all_gather x1, waiting for transfers between devices: 0.01 us -> 118 us  [body(): col_modes = lax.all_gather(modes, 'row', axis=1, tiled=True)]
    all_to_all x1, waiting for transfers between devices: 172 us -> 91.6 us  [body(): lax.all_to_all(outgoing, ('row', 'col'), split_axis=0, concat_axis=0, til...]
    psum x1 -> x0, waiting for transfers between devices: 29.6 us -> none  [broadcast(): return lax.psum(kept, axis)]
    reduce_sum x0 -> x1, other arithmetic: none -> 12 us  [summed_here(): result = parts.sum(axis=0)]
    unnamed x16 -> x20, local copies, waits for them, and re-layouts: 16.4 us -> 12.3 us
  transfers between devices with their start and end apart: 5 -> 5, of which waited for: 3 -> 3; matrix products, arithmetic and copies ran while one was open for 33% -> 34% of each run, Pallas kernels for 0% -> 0%
where the time goes in v1:
time: 692 us; the launch traced here: 686 us
  waiting for transfers between devices  360 us (52%)
  local copies, waits for them, and re-layouts  114 us (16%)
  matrix products  95.9 us (14%)
  other arithmetic  83.5 us (12%)
  between operations  14.9 us (2%)
  starting transfers between devices  11.5 us (2%)
    reduce_scatter x1, waiting for transfers between devices, body(): lax.psum_scatter(jnp.dot(left_modes.T, right_side, precision=lax.Precisio...  149 us
    all_gather x1, waiting for transfers between devices, body(): col_modes = lax.all_gather(modes, 'row', axis=1, tiled=True)  118 us
    all_to_all x1, waiting for transfers between devices, body(): lax.all_to_all(outgoing, ('row', 'col'), split_axis=0, concat_axis=0, til...  91.6 us
    slice x2, local copies, waits for them, and re-layouts, body(): mass_tile = full_pair[1]  39.5 us
    dot_general x1, matrix products, body(): jnp.dot(left_modes.T, right_side, precision=lax.Precision.HIGHEST, prefer...  35.7 us
    dot_general x1, matrix products, body(): jnp.dot(stiff_tile, col_modes, preferred_element_type=jnp.float32)  27.2 us
    dot_general x1, matrix products, body(): jnp.dot(mass_off, col_modes, preferred_element_type=jnp.float32)  23.5 us
    broadcast_in_dim x1, local copies, waits for them, and re-layouts, body(): jax.ops.segment_sum(arrived, jnp.maximum(arrived_slots, 0), num_segments=...  21.4 us
  transfers between devices with their start and end apart: 5, of which 3 were waited for; matrix products, arithmetic and copies ran while one was open for 34% of the time, Pallas kernels for 0%

profile of v1, /device:TPU:0, one launch (start us, length us, event | category | flops | bytes accessed | tf_op | source)
XLA Modules:
  0.0 686.3 jit_solution(8438299642687415313)
XLA Ops:
  11.9 7.3 %all-to-all-start = ((s32[32,1,1]{2,1,0:T(1,128)}), s32[32,1,1]{2,1,0:T(1,128)S(1)}, u32[]{:S(2)}, u32[]{:S(2)}) async-start(s32[32,1,1]{2,1,0:T(1,128)} %copy.25), calls=%async_computation | async-start | bytes 32768 | tf_op jit(solution)/shard_map/all_to_all | solution.py:68
  19.4 118.4 %all-gather.4.cloned.1.call-done = bf16[4096,1024]{1,0:T(8,128)(2,1)} async-done(((bf16[4096,128]{1,0:T(8,128)(2,1)}), bf16[4096,1024]{1,0:T(8,128)(2,1)}) %all-gather.4.cloned.1.call-update) | async-done | bytes 8388624 | tf_op jit(solution)/shard_map/all_gather | solution.py:85
  137.8 5.3 dynamic-slice_select_fusion
  143.2 15.2 %while.10 = (s32[]{:T(128)}, f32[2,2,512,512]{3,2,1,0:T(8,128)}, bf16[2,512,512]{2,1,0:T(8,128)(2,1)S(1)}, bf16[2,1024,512]{2,1,0:T(8,128)(2,1)S(1)}, bf16[2,102...) while((s32[]{:T(128)}, f32[2,2,512,512]{3,2,1,0:T(8,128)}, ...), condition=%wide.region_3.4_spmd, body=%wide.region_2.3_spmd.sunk | while | flops 2151940096 | bytes 47730848 | solution.py:50
  158.4 5.3 reshape.158
  163.7 4.8 copy.26
  168.5 5.0 gather_fusion.1
  173.5 5.1 select_multiply_fusion
  184.7 91.6 %all-to-all-done.1 = f32[32,2,128,128]{3,2,1,0:T(8,128)} async-done(((f32[32,2,128,128]{3,2,1,0:T(8,128)}), f32[32,2,128,128]{3,2,1,0:T(8,128)}, u32[]{:S(2)}, u32[]{:S(2)}) %all-to-all-start.1) | async-done | bytes 4194336 | tf_op jit(solution)/shard_map/all_to_all | solution.py:67
  276.2 21.4 %broadcast_in_dim.82 = f32[512,2,128,128]{3,2,1,0:T(8,128)} broadcast(f32[]{:T(128)} %constant.134.clone.1), dimensions={} | broadcast | bytes 67108864 | tf_op jit(solution)/shard_map/broadcast_in_dim | solution.py:70
  297.6 9.7 %scatter_fusion = f32[512,2,128,128]{3,2,1,0:T(8,128)} fusion(f32[512,2,128,128]{3,2,1,0:T(8,128)} %broadcast_in_dim.82, s32[32]{0:T(128)S(1)} %maximum_reduce_fusion, f32[32,2,128,128]{3,2,1,0:T(8,128)} %all-to-all-done.1), kind=kCustom, calls=%fused_computation.2 | custom fusion | flops 1048576 | bytes 12583040 | tf_op jit(solution)/shard_map/scatter-add | solution.py:70
  307.4 27.9 %fusion.25 = (bf16[1,16,128,32,128]{4,2,0,3,1:T(8,128)(2,1)S(1)}, bf16[1,16,128,32,128]{4,2,0,3,1:T(8,128)(2,1)}) fusion(f32[2,16,128,32,128]{4,2,0,3,1:T(8,128)} %bitcast.12), kind=kLoop, calls=%fused_computation.65 | loop fusion | bytes 67108864 | tf_op jit(solution)/shard_map/slice | solution.py:80
  335.3 14.7 %copy.27 = bf16[1,16,128,32,128]{4,3,2,1,0:T(8,128)(2,1)S(1)} copy(bf16[1,16,128,32,128]{4,2,0,3,1:T(8,128)(2,1)} %get-tuple-element.62) | data formatting | bytes 33554432 | tf_op jit(solution)/shard_map/slice | solution.py:83
  350.0 11.0 %copy.35 = bf16[256,8,32,128]{3,1,2,0:T(8,128)(2,1)} copy(bf16[256,8,32,128]{3,2,1,0:T(8,128)(2,1)S(1)} %bitcast.77) | data formatting | bytes 33554432
  361.0 11.6 %copy.28 = bf16[1,16,128,32,128]{4,3,2,1,0:T(8,128)(2,1)} copy(bf16[1,16,128,32,128]{4,2,0,3,1:T(8,128)(2,1)S(1)} %get-tuple-element.61) | data formatting | bytes 33554432 | tf_op jit(solution)/shard_map/slice | solution.py:80
  372.6 14.6 %select_reduce_fusion = f32[16,128]{1,0:T(8,128)S(1)} fusion(s32[16,128]{1,0:T(8,128)S(1)} %add_add_fusion, s32[32,128]{1,0:T(8,128)S(1)} %multiply_add_fusion, pred[]{:T(512)S(6)} %eq.67, f32[2,16,128,32,128]{4,2,0,3,1:T(8,128)} %bitcast.12), kind=kLoop, calls=%fused_computation.28 | loop fusion | flops 33552384 | bytes 33587200 | tf_op jit(solution)/shard_map/reduce_sum | solution.py:81
  387.2 6.6 all-reduce
  393.8 21.1 %fusion.17 = bf16[2048,4096]{1,0:T(8,128)(2,1)} fusion(bf16[256,8,32,128]{3,2,1,0:T(8,128)(2,1)} %bitcast.76, s32[2048]{0:T(1024)S(1)} %iota_add_fusion, pred[]{:T(512)S(6)} %eq.67), kind=kLoop, calls=%fused_computation.26 | loop fusion | flops 25165824 | bytes 33562624 | tf_op jit(solution)/shard_map/convert_element_type | solution.py:84
  414.9 23.5 %fusion.28 = f32[2048,1024]{0,1:T(8,128)S(1)} fusion(bf16[2048,4096]{1,0:T(8,128)(2,1)} %fusion.17, bf16[4096,1024]{1,0:T(8,128)(2,1)} %all-gather.4.cloned.1.call-done), kind=kOutput, calls=%fused_computation.68 | convolution fusion | flops 17179869184 | bytes 33554432 | tf_op jit(solution)/shard_map/dot_general | solution.py:93
  438.4 27.2 %fusion.27 = f32[2048,1024]{0,1:T(8,128)} fusion(bf16[2048,4096]{1,0:T(8,128)(2,1)} %bitcast.79, bf16[4096,1024]{1,0:T(8,128)(2,1)} %all-gather.4.cloned.1.call-done), kind=kOutput, calls=%fused_computation.67 | convolution fusion | flops 17179869184 | bytes 33554432 | tf_op jit(solution)/shard_map/dot_general | solution.py:92
  465.6 10.0 %pad_maximum_fusion = f32[2048,2048]{0,1:T(8,128)} fusion(f32[2048,1024]{0,1:T(8,128)S(1)} %fusion.28, f32[2048,1024]{0,1:T(8,128)} %fusion.27), kind=kLoop, calls=%fused_computation.32 | loop fusion | flops 4194304 | bytes 33554432 | tf_op jit(solution)/shard_map/concatenate | solution.py:90
  475.6 12.0 %reduce_sum.23 = bf16[2048,1024]{1,0:T(8,128)(2,1)} reduce(bf16[4,2048,1024]{2,1,0:T(8,128)(2,1)} %bitcast.78, bf16[]{:T(256)} %constant.153.clone.1), dimensions={0}, to_apply=%region_5.6 | reduce | flops 6291456 | bytes 20971522 | tf_op jit(solution)/shard_map/reduce_sum | solution.py:11
  493.1 35.7 %fusion.29 = f32[1024,2048]{1,0:T(8,128)} fusion(bf16[2048,1024]{1,0:T(8,128)(2,1)S(1)} %copy-done.1, f32[2048,2048]{0,1:T(8,128)} %fusion.21), kind=kOutput, calls=%fused_computation.69 | convolution fusion | flops 51539607552 | bytes 29360128 | tf_op jit(solution)/shard_map/dot_general | solution.py:109
  528.8 149.0 %reduce-scatter.2.cloned.1.call-done = f32[32,2048]{1,0:T(8,128)} async-done(((f32[1024,2048]{1,0:T(8,128)}), f32[32,2048]{1,0:T(8,128)}) %reduce-scatter.2.cloned.1.call-update) | async-done | bytes 262160 | tf_op jit(solution)/shard_map/reduce_scatter | solution.py:108
  (69 shorter events, 32.4 us)
Async XLA Ops:
  7.2 136.0 %copy-start.8 = (bf16[2,512,512]{2,1,0:T(8,128)(2,1)S(1)}, bf16[2,512,512]{2,1,0:T(8,128)(2,1)}, u32[]{:S(2)}) copy-start(bf16[2,512,512]{2,1,0:T(8,128)(2,1)} %param.11) | copy-start | bytes 3145732
  7.2 136.0 %copy-start.7 = (bf16[2,1024,512]{2,1,0:T(8,128)(2,1)S(1)}, bf16[2,1024,512]{2,1,0:T(8,128)(2,1)}, u32[]{:S(2)}) copy-start(bf16[2,1024,512]{2,1,0:T(8,128)(2,1)} %param.10) | copy-start | bytes 6291460
  7.2 136.0 %copy-start.4 = (f32[2,1024]{1,0:T(2,128)S(1)}, f32[2,1024]{1,0:T(2,128)}, u32[]{:S(2)}) copy-start(f32[2,1024]{1,0:T(2,128)} %param.12) | copy-start | bytes 24580
  7.2 136.0 %copy-start.5 = (f32[2,512]{1,0:T(2,128)S(1)}, f32[2,512]{1,0:T(2,128)}, u32[]{:S(2)}) copy-start(f32[2,512]{1,0:T(2,128)} %param.13) | copy-start | bytes 12292
  7.2 130.5 %all-gather.4.cloned.1.call-start = ((), (), s32[]{:S(2)}) async-start(), calls=%async_computation.3 | async-start | bytes 9437184 | tf_op jit(solution)/shard_map/all_gather | solution.py:85
  11.9 166.7 %all-to-all-start = ((s32[32,1,1]{2,1,0:T(1,128)}), s32[32,1,1]{2,1,0:T(1,128)S(1)}, u32[]{:S(2)}, u32[]{:S(2)}) async-start(s32[32,1,1]{2,1,0:T(1,128)} %copy.25), calls=%async_computation | async-start | bytes 32768 | tf_op jit(solution)/shard_map/all_to_all | solution.py:68
  19.3 456.3 %all-gather.6.cloned.1.call-start = ((), (), s32[]{:S(2)}) async-start(), calls=%async_computation.5 | async-start | bytes 20971520 | tf_op jit(solution)/shard_map/all_gather | solution.py:10
  143.2 4.7 copy-start.2
  148.1 2.2 copy-start.3
  150.3 5.0 copy-start.2
  155.6 2.8 copy-start.3
  173.5 9.2 %copy-start.9 = (u32[32]{0:T(128)S(1)}, u32[32]{0:T(128)}, u32[]{:S(2)}) copy-start(u32[32]{0:T(128)} %constant.165) | copy-start | bytes 388
  178.6 97.6 %all-to-all-start.1 = ((f32[32,2,128,128]{3,2,1,0:T(8,128)}), f32[32,2,128,128]{3,2,1,0:T(8,128)}, u32[]{:S(2)}, u32[]{:S(2)}) async-start(f32[32,2,128,128]{3,2,1,0:T(8,128)} %select_multiply_fusion), calls=%async_computation.1 | async-start | bytes 8388608 | tf_op jit(solution)/shard_map/all_to_all | solution.py:67
  182.2 495.6 %reduce-scatter.2.cloned.1.call-start = ((), (), s32[]{:S(2)}) async-start(), calls=%async_computation.4 | async-start | bytes 8650752 | tf_op jit(solution)/shard_map/reduce_scatter | solution.py:108
  393.8 95.7 %copy-start.6 = (f32[512]{0:T(512)}, f32[512]{0:T(512)S(1)}, u32[]{:S(2)}) copy-start(f32[512]{0:T(512)S(1)} %dynamic-slice.1) | copy-start | bytes 6148
  438.4 27.2 %copy-start = (f32[2048,1024]{0,1:T(8,128)}, f32[2048,1024]{0,1:T(8,128)S(1)}, u32[]{:S(2)}) copy-start(f32[2048,1024]{0,1:T(8,128)S(1)} %fusion.28) | copy-start | bytes 25165828
  489.5 3.5 copy-start.1
Sparse Core Ops, SparseCore 0:
  10.1 127.6 all-gather.3
  143.2 149.0 all-gather.5
  528.9 148.8 reduce-scatter.1
